TPU v7x, 32 devices: a whole 2x2x4 slice. The times are simulated.
32 devices in a mesh: dp: 8 (over z, y), tm: 4 (over x, core).
Axes of the slice: x: 2, y: 2, z: 4, core: 2. Of those that a mesh axis runs over, the one named last changes fastest.
Arguments:
- latents: bfloat16 [8, 16, 16, 16, 640], P('dp', 'tm'), may hold values from -60 to 60
- cotangent: bfloat16 [8, 8, 16, 16, 640], P('dp', 'tm'), may hold values from -6 to 6
- timesteps: int32 [8], P('dp'), may hold values from 0 to 999
- spatial_weight: bfloat16 [640, 5760], P('dp'), may hold values from -0.078125 to 0.078125
- temporal_weight: bfloat16 [640, 1920], P('dp'), may hold values from -0.125 to 0.125
- time_weight: bfloat16 [640, 256], P('dp'), may hold values from -0.375 to 0.375
Outputs:
- downsampled: float32 [8, 8, 16, 16, 640], P('dp', 'tm')
- latents_grad: float32 [8, 16, 16, 16, 640], P('dp', 'tm')
- spatial_grad: float32 [640, 5760], P('dp')
- temporal_grad: float32 [640, 1920], P('dp')
- time_grad: float32 [640, 256], P('dp')
All inputs are finite; a program needn't handle non-finite values.
Results may differ from a plain program's by a relative error of at most 0.0041.
Values may be sent and summed in bfloat16 or wider, within the bound.
No kernel may reach another device: no remote copies, remote signals or barrier semaphores. Data moves between devices by JAX's collectives and lax.ppermute only.
A program may use at most 128 MiB of HBM per device.

v0:
```python
import math
import jax
import jax.numpy as jnp
from jax import lax
from jax.sharding import PartitionSpec as P

GROUPS = 32
epsilon = 1e-05
log_base = math.log(10000.0)


def from_behind(x, axis, by):
    count = lax.axis_size(axis)
    pairs = [(i, i + by) for i in range(count) if 0 <= i + by < count]
    return lax.ppermute(x, axis, pairs)


def embedding(diffusion_step, embed_width):
    half_width = embed_width // 2
    frequency = jnp.exp(-log_base * jnp.arange(half_width, dtype=jnp.float32) / half_width)
    angles = diffusion_step.astype(jnp.float32) * frequency
    return jnp.concatenate([jnp.cos(angles), jnp.sin(angles)])


def normalize(frames):
    frame_count, height, breadth, channels = frames.shape
    grouped = frames.astype(jnp.float32).reshape(
        frame_count, height * breadth, GROUPS, channels // GROUPS
    )
    center = jnp.mean(grouped, axis=(1, 3), keepdims=True)
    deviation = grouped - center
    variance = jnp.mean(deviation * deviation, axis=(1, 3), keepdims=True)
    scaled = lax.rsqrt(variance + epsilon)
    return (deviation * scaled, scaled)


def spatial_columns(activation):
    frame_count, height, breadth, channels = activation.shape
    padded = jnp.pad(activation, ((0, 0), (1, 1), (1, 1), (0, 0)))
    shifted_views = [
        padded[:, row_shift : row_shift + height, col_shift : col_shift + breadth, :]
        for row_shift in range(3)
        for col_shift in range(3)
    ]
    return jnp.stack(shifted_views, axis=3).reshape(frame_count * height * breadth, 9, channels)


def spatial_fold(pieces, frame_count, height, breadth):
    channels = pieces.shape[-1]
    layout = pieces.reshape(frame_count, height, breadth, 9, channels)
    total = jnp.zeros((frame_count, height + 2, breadth + 2, channels), jnp.float32)
    for row_shift in range(3):
        for col_shift in range(3):
            placed = jnp.pad(
                layout[:, :, :, 3 * row_shift + col_shift, :],
                ((0, 0), (row_shift, 2 - row_shift), (col_shift, 2 - col_shift), (0, 0)),
            )
            total = total + placed
    return total[:, 1 : height + 1, 1 : breadth + 1, :]


def temporal_columns(extended):
    out_count = (extended.shape[0] - 1) // 2
    taps = [extended[offset : offset + 2 * out_count : 2] for offset in range(3)]
    return jnp.stack(taps, axis=2).reshape(out_count * extended.shape[1], 3, extended.shape[2])


def temporal_back(parts, incoming):
    lead_tap = parts[:, :, 0, :]
    mid_tap = parts[:, :, 1, :]
    tail_tap = parts[:, :, 2, :]
    even_frames = jnp.concatenate([lead_tap[1:], incoming[None]], axis=0) + tail_tap
    merged = jnp.stack([mid_tap, even_frames], axis=1)
    return (merged.reshape(2 * parts.shape[0], parts.shape[1], parts.shape[3]), lead_tap[0])


def spatial_forward(frames, spatial_taps, time_shift):
    frame_count, height, breadth, channels = frames.shape
    normal, scaled = normalize(frames)
    activation = (
        jax.nn.silu(normal).reshape(frame_count, height, breadth, channels).astype(jnp.bfloat16)
    )
    columns = spatial_columns(activation)
    conv_sum = (
        jnp.einsum("rkc,ckq->rq", columns, spatial_taps, preferred_element_type=jnp.float32)
        + time_shift
    )
    hidden = conv_sum.astype(jnp.bfloat16).reshape(frame_count, height * breadth, channels)
    return (hidden, normal, scaled, columns)


def body(latents, cotangent, timesteps, spatial_weight, temporal_weight, time_weight):
    clip_frames = latents[0]
    frame_count, height, breadth, channels = clip_frames.shape
    pixels = height * breadth
    out_count = frame_count // 2
    spatial_full, temporal_full, time_full = (
        lax.all_gather(spatial_weight, "dp", axis=0, tiled=True),
        lax.all_gather(temporal_weight, "dp", axis=0, tiled=True),
        lax.all_gather(time_weight, "dp", axis=0, tiled=True),
    )
    spatial_taps = spatial_full.reshape(channels, 9, channels)
    temporal_taps = temporal_full.reshape(channels, 3, channels)
    embedded = embedding(timesteps[0], time_full.shape[1])
    time_shift = jnp.dot(time_full.astype(jnp.float32), embedded, precision=lax.Precision.HIGHEST)
    hidden, normal, scaled, columns = spatial_forward(clip_frames, spatial_taps, time_shift)
    before = from_behind(hidden[-1], "tm", 1)
    extended = jnp.concatenate([before[None], hidden], axis=0)
    tcols = temporal_columns(extended)
    result = jnp.einsum("rkc,ckq->rq", tcols, temporal_taps, preferred_element_type=jnp.float32)
    downsampled = result.reshape(1, out_count, height, breadth, channels)
    grad_out = cotangent[0].reshape(out_count * pixels, channels)
    parts = jnp.einsum(
        "rq,ckq->rkc", grad_out, temporal_taps, preferred_element_type=jnp.float32
    ).reshape(out_count, pixels, 3, channels)
    local_grad, leaving = temporal_back(parts, jnp.zeros((pixels, channels), jnp.float32))
    arriving = from_behind(leaving, "tm", -1)
    hidden_grad = local_grad.at[-1].add(arriving)
    hidden_back = hidden_grad.astype(jnp.bfloat16).reshape(frame_count * pixels, channels)
    shift_grad = jnp.sum(hidden_grad, axis=(0, 1))
    pieces = jnp.einsum(
        "rq,ckq->rkc", hidden_back, spatial_taps, preferred_element_type=jnp.float32
    )
    activation_grad = spatial_fold(pieces, frame_count, height, breadth)
    sigmoid_value = jax.nn.sigmoid(normal)
    derivative = sigmoid_value * (1.0 + normal * (1.0 - sigmoid_value))
    norm_grad = activation_grad.reshape(normal.shape) * derivative
    mean_one = jnp.mean(norm_grad, axis=(1, 3), keepdims=True)
    mean_two = jnp.mean(norm_grad * normal, axis=(1, 3), keepdims=True)
    input_grad = ((norm_grad - mean_one - normal * mean_two) * scaled).reshape(
        1, frame_count, height, breadth, channels
    )
    row_share = channels // lax.axis_size("dp")
    spatial_part = jnp.einsum(
        "rkc,rq->ckq", columns, hidden_back, preferred_element_type=jnp.float32
    )
    temporal_part = jnp.einsum("rkc,rq->ckq", tcols, grad_out, preferred_element_type=jnp.float32)
    time_part = shift_grad[:, None] * embedded[None, :]
    grad_shard = lax.psum_scatter(
        jnp.concatenate(
            [
                spatial_part.reshape(row_share * lax.axis_size("dp"), 9 * channels),
                temporal_part.reshape(row_share * lax.axis_size("dp"), 3 * channels),
                time_part,
            ],
            axis=1,
        ),
        "dp",
        scatter_dimension=0,
        tiled=True,
    )
    totals = lax.psum(grad_shard, "tm")
    spatial_grad = totals[:, : 9 * channels]
    temporal_grad = totals[:, 9 * channels : 12 * channels]
    time_grad = totals[:, 12 * channels :]
    return (downsampled, input_grad, spatial_grad, temporal_grad, time_grad)


def solution(mesh):
    placed = (
        P("dp", "tm", None, None, None),
        P("dp", "tm", None, None, None),
        P("dp"),
        P("dp", None),
        P("dp", None),
        P("dp", None),
    )
    return jax.shard_map(
        body,
        mesh=mesh,
        in_specs=placed,
        out_specs=(
            P("dp", "tm", None, None, None),
            P("dp", "tm", None, None, None),
            P("dp", None),
            P("dp", None),
            P("dp", None),
        ),
        check_vma=False,
    )
```

profile of v0, /device:TPU:0, one launch (start us, length us, event | category | flops | bytes accessed | tf_op | source)
XLA Modules:
  0.0 723.6 jit_solution(1900016296076289256)
XLA Ops:
  7.2 0.7 all-gather.5.cloned.1.call-update
  8.0 0.7 all-gather.3.cloned.1.call-update
  8.7 1.5 convert_reduce_fusion
  10.5 0.1 sub.59
  10.7 0.4 multiply_reduce_fusion.1
  11.4 0.1 mul.122
  12.2 33.4 %all_gather.10 = bf16[640,256]{1,0:T(8,128)(2,1)S(1)} all-gather(bf16[80,256]{1,0:T(8,128)(2,1)S(1)} %copy-done.14), channel_id=1, replica_groups=mesh['dp'=8,'tm'=4] {'dp'}, dimensions={0}, use_global_device_ids=true | all-gather | bytes 368640 | tf_op jit(solution)/shard_map/all_gather | solution.py:100
  45.6 0.4 convolution_reduce_fusion
  46.0 20.7 %all-gather.5.cloned.1.call-done = bf16[640,1920]{1,0:T(8,128)(2,1)} async-done(((bf16[80,1920]{1,0:T(8,128)(2,1)}), bf16[640,1920]{1,0:T(8,128)(2,1)}) %all-gather.5.cloned.1.call-update) | async-done | bytes 2457616 | tf_op jit(solution)/shard_map/all_gather | solution.py:99
  66.7 4.3 copy.34
  71.0 3.4 fusion.18
  74.5 1.5 collective-permute-start.1
  76.2 0.2 pad_maximum_fusion.1
  76.4 0.2 copy.39
  76.6 1.9 collective-permute-done.1
  78.5 0.1 fusion.8
  78.7 0.3 fusion.13
  79.0 1.2 broadcast_multiply_fusion
  80.2 100.1 %all-gather.3.cloned.1.call-done = bf16[640,5760]{1,0:T(8,128)(2,1)} async-done(((bf16[80,5760]{1,0:T(8,128)(2,1)}), bf16[640,5760]{1,0:T(8,128)(2,1)}) %all-gather.3.cloned.1.call-update) | async-done | bytes 7372816 | tf_op jit(solution)/shard_map/all_gather | solution.py:98
  180.3 10.3 %copy.32 = bf16[640,5760]{0,1:T(8,128)(2,1)} copy(bf16[640,5760]{1,0:T(8,128)(2,1)} %all-gather.3.cloned.1.call-done) | data formatting | bytes 14745600 | tf_op jit(solution)/shard_map/all_gather | solution.py:98
  190.6 15.7 %fusion.16 = f32[1024,640,9]{1,0,2:T(8,128)} fusion(bf16[1024,640,1]{1,0,2:T(8,128)(2,1)S(1)} %bitcast.165, bf16[640,9,640]{0,2,1:T(8,128)(2,1)} %bitcast.137), kind=kOutput, calls=%fused_computation.78 | convolution fusion | flops 7549747200 | bytes 32276480 | tf_op jit(solution)/shard_map/rq,ckq->rkc/dot_general | solution.py:121
  206.2 13.8 %slice_bitcast_fusion.8 = (f32[4,16,16,640]{3,2,1,0:T(8,128)}, f32[4,16,16,640]{3,2,1,0:T(8,128)S(1)}, f32[4,16,16,640]{3,2,1,0:T(8,128)S(1)}, f32[4,16,16,640]{...) fusion(f32[4,16,16,9,640]{4,2,1,0,3:T(8,128)} %bitcast.132), kind=kLoop, calls=%fused_computation.24 | loop fusion | bytes 47185920 | tf_op jit(solution)/shard_map/squeeze | solution.py:55
  220.1 4.2 pad_add_fusion
  224.3 0.6 copy-done.3
  224.9 0.8 copy-done.4
  225.7 3.8 multiply_multiply_fusion
  229.4 1.0 fusion.12
  230.5 3.0 pad_slice_fusion
  233.5 0.1 constant_dynamic-update-slice_fusion.8
  233.6 0.2 constant_dynamic-update-slice_fusion.7
  233.9 0.2 constant_dynamic-update-slice_fusion.6
  234.1 0.2 constant_dynamic-update-slice_fusion.5
  234.3 0.2 mul.123
  234.5 0.2 sub.60
  234.7 0.8 constant_dynamic-update-slice_fusion.4
  235.6 4.4 copy-done.13
  239.9 1.2 constant_dynamic-update-slice_fusion.3
  241.1 1.2 constant_dynamic-update-slice_fusion.2
  242.3 1.2 constant_dynamic-update-slice_fusion.1
  243.5 1.2 constant_dynamic-update-slice_fusion
  244.6 12.7 %fusion.3 = bf16[1024,640]{1,0:T(8,128)(2,1)S(1)} fusion(bf16[1024,9,640]{2,0,1:T(8,128)(2,1)} %constant_dynamic-update-slice_fusion, bf16[640,9,640]{0,2,1:T(8,128)(2,1)S(1)} %bitcast.140, f32[640]{0:T(1024)S(1)} %convolution_reduce_fusion), kind=kOutput, calls=%fused_computation.31 | convolution fusion | flops 7551057920 | bytes 20482560 | tf_op jit(solution)/shard_map/rkc,ckq->rq/dot_general | solution.py:85
  257.4 0.8 slice.149
  258.1 2.1 collective-permute-start
  260.2 15.0 %fusion.17 = f32[640,9,640]{2,0,1:T(8,128)} fusion(bf16[1024,640,1]{1,0,2:T(8,128)(2,1)S(1)} %bitcast.166, bf16[1024,9,640]{2,0,1:T(8,128)(2,1)} %constant_dynamic-update-slice_fusion), kind=kOutput, calls=%fused_computation.79 | convolution fusion | flops 7549747200 | bytes 27852800 | tf_op jit(solution)/shard_map/rkc,rq->ckq/dot_general | solution.py:134
  275.2 15.1 %copy.44 = f32[640,5760]{1,0:T(8,128)} copy(f32[640,5760]{0,1:T(8,128)} %bitcast.133) | data formatting | bytes 29491200 | tf_op jit(solution)/shard_map/reshape | solution.py:142
  290.3 0.1 fusion.14
  290.5 1.4 pad_maximum_fusion.3
  291.9 3.9 fusion.11
  295.8 6.0 copy.45
  301.8 15.2 %pad_maximum_fusion = f32[640,7936]{1,0:T(8,128)} fusion(f32[640,256]{1,0:T(8,128)S(1)} %copy-done.9, f32[640,1920]{1,0:T(8,128)} %copy.45, f32[640,5760]{1,0:T(8,128)} %copy.44), kind=kLoop, calls=%fused_computation | loop fusion | flops 10158080 | bytes 40632320 | tf_op jit(solution)/shard_map/concatenate | solution.py:140
  317.4 0.1 mul.141
  317.5 0.1 reduce_sum.80
  317.8 0.1 sub.69
  317.9 332.6 %reduce-scatter.2.cloned.1.call-done = f32[80,7936]{1,0:T(8,128)} async-done(((f32[640,7936]{1,0:T(8,128)}), f32[80,7936]{1,0:T(8,128)}) %reduce-scatter.2.cloned.1.call-update) | async-done | bytes 2539536 | tf_op jit(solution)/shard_map/reduce_scatter | solution.py:139
  650.5 4.7 fusion.2
  655.3 0.3 pad_maximum_fusion.2
  655.5 1.4 copy-done.10
  656.9 1.8 fusion.15
  658.8 0.1 copy.61
  658.9 1.1 copy.46
  660.0 50.8 %all-reduce.13.cloned.1.call-done = f32[80,7936]{1,0:T(8,128)} async-done(((f32[80,7936]{1,0:T(8,128)}), f32[80,7936]{1,0:T(8,128)}) %all-reduce.13.cloned.1.call-update) | async-done | bytes 2539536 | tf_op jit(solution)/shard_map/psum | solution.py:152
  710.8 2.9 slice.165
  713.6 1.9 slice.166
  715.6 1.5 slice.167
  (59 shorter events, 1.7 us)
Async XLA Ops:
  7.2 63.8 %copy-start = (bf16[1,2,16,16,640]{4,3,2,1,0:T(8,128)(2,1)S(1)}, bf16[1,2,16,16,640]{4,3,2,1,0:T(8,128)(2,1)}, u32[]{:S(2)}) copy-start(bf16[1,2,16,16,640]{4,3,2,1,0:T(8,128)(2,1)} %param.9) | copy-start | bytes 1966084
  7.2 3.5 copy-start.1
  7.2 5.0 copy-start.14
  7.2 59.5 %all-gather.5.cloned.1.call-start = ((), (), s32[]{:S(2)}) async-start(), calls=%async_computation.2 | async-start | bytes 2764800 | tf_op jit(solution)/shard_map/all_gather | solution.py:99
  7.9 172.4 %all-gather.3.cloned.1.call-start = ((), (), s32[]{:S(2)}) async-start(), calls=%async_computation.1 | async-start | bytes 8294400 | tf_op jit(solution)/shard_map/all_gather | solution.py:98
  8.7 641.8 %reduce-scatter.2.cloned.1.call-start = ((), (), s32[]{:S(2)}) async-start(), calls=%async_computation.3 | async-start | bytes 22855680 | tf_op jit(solution)/shard_map/reduce_scatter | solution.py:139
  74.5 4.0 collective-permute-start.1
  79.0 111.6 %copy-start.11 = (bf16[4,256,640]{2,1,0:T(8,128)(2,1)}, bf16[4,256,640]{2,1,0:T(8,128)(2,1)S(1)}, u32[]{:S(2)}) copy-start(bf16[4,256,640]{2,1,0:T(8,128)(2,1)S(1)} %get-tuple-element.38) | copy-start | bytes 3932164
  220.0 4.3 copy-start.2
  220.0 4.8 copy-start.3
  220.0 5.6 copy-start.4
  234.7 9.9 %slice-start = ((s8[7372800]{0:T(1024)(128)(4,1)}), s8[4194304]{0:T(1024)(128)(4,1)S(1)}, s32[]{:S(2)}) async-start(s8[7372800]{0:T(1024)(128)(4,1)} %bitcast.138), calls=%async_computation.5 | async-start | bytes 8388608
  235.6 4.4 copy-start.13
  239.9 4.7 slice-start.1
  244.6 15.6 %copy-start.12 = (bf16[4,256,640]{2,1,0:T(8,128)(2,1)S(1)}, bf16[4,256,640]{2,1,0:T(8,128)(2,1)}, u32[]{:S(2)}) copy-start(bf16[4,256,640]{2,1,0:T(8,128)(2,1)} %copy-done.11) | copy-start | bytes 3932164
  258.1 32.3 %collective-permute-start = (bf16[256,640]{1,0:T(8,128)(2,1)}, bf16[256,640]{1,0:T(8,128)(2,1)}, u32[]{:S(2)}, u32[]{:S(2)}) collective-permute-start(bf16[256,640]{1,0:T(8,128)(2,1)} %slice.149), channel_id=1, source_target_pairs={{0,1},{1,2},{2,3},{4,5},{5,6},{6,7},{8,9},{9,10},{10,11},{12,13},{... | collective-permute-start | bytes 983048 | tf_op jit(solution)/shard_map/ppermute | solution.py:15
  290.4 5.4 copy-start.5
  290.5 5.4 copy-start.7
  295.8 6.0 copy-start.9
  317.0 393.8 %all-reduce.13.cloned.1.call-start = ((), (), s32[]{:S(2)}) async-start(), calls=%async_computation.4 | async-start | bytes 5079040 | tf_op jit(solution)/shard_map/psum | solution.py:152
  650.5 4.7 copy-start.6
  650.5 4.7 copy-start.8
  655.3 1.7 copy-start.10
Sparse Core Ops, SparseCore 0:
  10.2 56.4 all-gather.4
  68.9 111.3 all-gather.2
  317.1 333.2 reduce-scatter.1
  652.9 57.8 all-reduce.12
where the time goes:
time: 725 us; the launch traced here: 724 us
  waiting for transfers between devices  508 us (70%)
  local copies, waits for them, and re-layouts  75.6 us (10%)
  matrix products  52.9 us (7%)
  other arithmetic  35.7 us (5%)
  blocking collectives  33.4 us (5%)
  between operations  14.9 us (2%)
    reduce_scatter x1, waiting for transfers between devices, body(): lax.psum_scatter(jnp.concatenate([spatial_part.reshape(row_share * lax.ax...  333 us
    all_gather x1, waiting for transfers between devices, body(): lax.all_gather(spatial_weight, 'dp', axis=0, tiled=True)  100 us
    psum x1, waiting for transfers between devices, body(): totals = lax.psum(grad_shard, 'tm')  50.8 us
    all_gather x1, blocking collectives, body(): lax.all_gather(time_weight, 'dp', axis=0, tiled=True)  33.4 us
    all_gather x1, waiting for transfers between devices, body(): lax.all_gather(temporal_weight, 'dp', axis=0, tiled=True)  20.7 us
    dot_general x1, matrix products, body(): jnp.einsum('rq,ckq->rkc', hidden_back, spatial_taps, preferred_element_ty...  15.7 us
    concatenate x1, other arithmetic, body(): jnp.concatenate([spatial_part.reshape(row_share * lax.axis_size('dp'), 9...  15.2 us
    reshape x1, local copies, waits for them, and re-layouts, body(): spatial_part.reshape(row_share * lax.axis_size('dp'), 9 * channels)  15.1 us
  transfers between devices with their start and end apart: 6, of which 5 were waited for; matrix products, arithmetic and copies ran while one was open for 7% of the time, Pallas kernels for 0%

commit v1 on v0

--- a/solution.py
+++ b/solution.py
@@ -7,6 +7,30 @@
 GROUPS = 32
 epsilon = 1e-05
 log_base = math.log(10000.0)
+
+
+def columns_put(base_x, array_axis):
+    base_x = jnp.moveaxis(base_x, 0, array_axis)
+    small = base_x.shape
+    outer = base_x.reshape(
+        *small[:array_axis], small[array_axis] * small[array_axis + 1], *small[array_axis + 2 :]
+    )
+    return outer
+
+
+def touch_the_tiles(target, axis_name):
+    y = lax.axis_size(axis_name)
+    u1 = lax.axis_index(axis_name)
+    part_now, found_now = (y, u1)
+    block_next, opened = (target[None], 1)
+    while opened < part_now:
+        even = lax.ppermute(block_next, axis_name, [(pp, pp ^ opened) for pp in range(part_now)])
+        next_value = found_now & opened == 0
+        h_now = jnp.where(next_value, block_next, even)
+        view_out = jnp.where(next_value, even, block_next)
+        block_next = jnp.concatenate([h_now, view_out])
+        opened *= 2
+    return block_next
 
 
 def from_behind(x, axis, by):
@@ -90,13 +114,19 @@
 
 
 def body(latents, cotangent, timesteps, spatial_weight, temporal_weight, time_weight):
+
+    def _use_squares(xin, patch, dim_i):
+        piece_next = touch_the_tiles(xin, patch)
+        current_block = columns_put(piece_next, dim_i)
+        return current_block
+
     clip_frames = latents[0]
     frame_count, height, breadth, channels = clip_frames.shape
     pixels = height * breadth
     out_count = frame_count // 2
     spatial_full, temporal_full, time_full = (
         lax.all_gather(spatial_weight, "dp", axis=0, tiled=True),
-        lax.all_gather(temporal_weight, "dp", axis=0, tiled=True),
+        _use_squares(temporal_weight, "dp", 0),
         lax.all_gather(time_weight, "dp", axis=0, tiled=True),
     )
     spatial_taps = spatial_full.reshape(channels, 9, channels)

time: 725 us -> 768 us (1.059)
  blocking collectives: 33.4 us -> 127 us
  waiting for transfers between devices: 508 us -> 433 us
  starting transfers between devices: 3.69 us -> 18.9 us
    all_gather x1, waiting for transfers between devices: 100 us -> 0.01 us  [body(): lax.all_gather(spatial_weight, 'dp', axis=0, tiled=True)]
    all_gather x1, blocking collectives: 33.4 us -> 127 us  [body(): lax.all_gather(time_weight, 'dp', axis=0, tiled=True)]
    ppermute x0 -> x3, waiting for transfers between devices: none -> 48.4 us  [touch_the_tiles(): lax.ppermute(block_next, axis_name, [(pp, pp ^ opened) for pp in range(pa...]
    all_gather x1 -> x0, waiting for transfers between devices: 20.7 us -> none  [body(): lax.all_gather(temporal_weight, 'dp', axis=0, tiled=True)]
    ppermute x2, starting transfers between devices: 3.53 us -> 11.9 us  [from_behind(): return lax.ppermute(x, axis, pairs)]
  transfers between devices with their start and end apart: 6 -> 8, of which waited for: 5 -> 5; matrix products, arithmetic and copies ran while one was open for 7% -> 8% of each run, Pallas kernels for 0% -> 0%
where the time goes in v1:
time: 768 us; the launch traced here: 767 us
  waiting for transfers between devices  433 us (56%)
  blocking collectives  127 us (17%)
  local copies, waits for them, and re-layouts  78.5 us (10%)
  matrix products  53.1 us (7%)
  other arithmetic  41.2 us (5%)
  starting transfers between devices  18.9 us (2%)
  between operations  14.8 us (2%)
    reduce_scatter x1, waiting for transfers between devices, body(): lax.psum_scatter(jnp.concatenate([spatial_part.reshape(row_share * lax.ax...  331 us
    all_gather x1, blocking collectives, body(): lax.all_gather(time_weight, 'dp', axis=0, tiled=True)  127 us
    psum x1, waiting for transfers between devices, body(): totals = lax.psum(grad_shard, 'tm')  50.7 us
    ppermute x3, waiting for transfers between devices, touch_the_tiles(): lax.ppermute(block_next, axis_name, [(pp, pp ^ opened) for pp in range(pa...  48.4 us
    dot_general x1, matrix products, body(): jnp.einsum('rq,ckq->rkc', hidden_back, spatial_taps, preferred_element_ty...  15.7 us
  transfers between devices with their start and end apart: 8, of which 5 were waited for; matrix products, arithmetic and copies ran while one was open for 8% of the time, Pallas kernels for 0%

profile of v1, /device:TPU:0, one launch (start us, length us, event | category | flops | bytes accessed | tf_op | source)
XLA Modules:
  0.0 766.8 jit_solution(15085166565373267573)
XLA Ops:
  7.2 0.7 all-gather.2.cloned.1.call-update
  8.0 3.0 collective-permute-start.1
  11.0 7.5 collective-permute-done.1
  18.5 1.0 broadcast_select_fusion.5
  19.5 0.7 copy-done.6
  20.3 1.9 collective-permute-start.2
  22.2 40.9 %collective-permute-done.2 = bf16[2,80,1920]{2,1,0:T(8,128)(2,1)} collective-permute-done((bf16[2,80,1920]{2,1,0:T(8,128)(2,1)S(1)}, bf16[2,80,1920]{2,1,0:T(8,128)(2,1)}, u32[]{:S(2)}, u32[]{:S(2)}) %collective-permute-start.2) | collective-permute-done | bytes 614432 | tf_op jit(solution)/shard_map/ppermute | solution.py:27
  63.1 1.3 broadcast_select_fusion.3
  64.4 1.2 pad_maximum_fusion.5
  65.5 2.0 collective-permute-start.3
  67.5 0.2 convert_reduce_fusion
  68.1 0.4 multiply_reduce_fusion.1
  69.7 127.4 %all_gather.7 = bf16[640,256]{1,0:T(8,128)(2,1)S(1)} all-gather(bf16[80,256]{1,0:T(8,128)(2,1)S(1)} %copy-done.15), channel_id=1, replica_groups=mesh['dp'=8,'tm'=4] {'dp'}, dimensions={0}, use_global_device_ids=true | all-gather | bytes 368640 | tf_op jit(solution)/shard_map/all_gather | solution.py:130
  197.1 0.4 convolution_reduce_fusion
  197.5 1.6 broadcast_select_fusion.1
  199.1 1.7 pad_maximum_fusion.2
  200.8 6.2 reshape_reshape.3
  206.9 3.7 fusion.8
  210.7 1.5 collective-permute-start.4
  212.4 0.2 pad_maximum_fusion.1
  212.6 0.2 copy.37
  212.8 1.9 collective-permute-done.4
  214.7 0.1 fusion.12
  214.9 0.3 fusion.17
  215.2 1.2 broadcast_multiply_fusion
  216.4 10.2 %copy.31 = bf16[640,5760]{0,1:T(8,128)(2,1)} copy(bf16[640,5760]{1,0:T(8,128)(2,1)} %all-gather.2.cloned.1.call-done) | data formatting | bytes 14745600 | tf_op jit(solution)/shard_map/all_gather | solution.py:128
  226.6 15.7 %fusion.19 = f32[1024,640,9]{1,0,2:T(8,128)} fusion(bf16[1024,640,1]{1,0,2:T(8,128)(2,1)S(1)} %bitcast.161, bf16[640,9,640]{0,2,1:T(8,128)(2,1)} %bitcast.134), kind=kOutput, calls=%fused_computation.90 | convolution fusion | flops 7549747200 | bytes 32276480 | tf_op jit(solution)/shard_map/rq,ckq->rkc/dot_general | solution.py:151
  242.3 13.8 %slice_bitcast_fusion.8 = (f32[4,16,16,640]{3,2,1,0:T(8,128)}, f32[4,16,16,640]{3,2,1,0:T(8,128)S(1)}, f32[4,16,16,640]{3,2,1,0:T(8,128)S(1)}, f32[4,16,16,640]{...) fusion(f32[4,16,16,9,640]{4,2,1,0,3:T(8,128)} %bitcast.129), kind=kLoop, calls=%fused_computation.24 | loop fusion | bytes 47185920 | tf_op jit(solution)/shard_map/squeeze | solution.py:79
  256.2 4.2 pad_add_fusion
  260.4 0.6 copy-done.3
  261.0 0.8 copy-done.4
  261.8 3.8 multiply_multiply_fusion
  265.6 1.0 fusion.16
  266.6 3.0 pad_slice_fusion
  269.7 0.2 constant_dynamic-update-slice_fusion.7
  270.0 0.2 constant_dynamic-update-slice_fusion.6
  270.2 0.2 constant_dynamic-update-slice_fusion.5
  270.4 0.2 mul.123
  270.6 0.2 sub.60
  270.8 0.8 constant_dynamic-update-slice_fusion.4
  271.7 4.4 copy-done.14
  276.0 1.2 constant_dynamic-update-slice_fusion.3
  277.2 1.2 constant_dynamic-update-slice_fusion.2
  278.4 1.2 constant_dynamic-update-slice_fusion.1
  279.6 1.2 constant_dynamic-update-slice_fusion
  280.8 12.7 %fusion.3 = bf16[1024,640]{1,0:T(8,128)(2,1)S(1)} fusion(bf16[1024,9,640]{2,0,1:T(8,128)(2,1)} %constant_dynamic-update-slice_fusion, bf16[640,9,640]{0,2,1:T(8,128)(2,1)S(1)} %bitcast.137, f32[640]{0:T(1024)S(1)} %convolution_reduce_fusion), kind=kOutput, calls=%fused_computation.31 | convolution fusion | flops 7551057920 | bytes 20482560 | tf_op jit(solution)/shard_map/rkc,ckq->rq/dot_general | solution.py:109
  293.6 0.8 slice.149
  294.3 10.5 %collective-permute-start = (bf16[256,640]{1,0:T(8,128)(2,1)}, bf16[256,640]{1,0:T(8,128)(2,1)}, u32[]{:S(2)}, u32[]{:S(2)}) collective-permute-start(bf16[256,640]{1,0:T(8,128)(2,1)} %slice.149), channel_id=1, source_target_pairs={{0,1},{1,2},{2,3},{4,5},{5,6},{6,7},{8,9},{9,10},{10,11},{12,13},{... | collective-permute-start | bytes 983048 | tf_op jit(solution)/shard_map/ppermute | solution.py:39
  304.8 14.9 %fusion.20 = f32[640,9,640]{2,0,1:T(8,128)} fusion(bf16[1024,640,1]{1,0,2:T(8,128)(2,1)S(1)} %bitcast.162, bf16[1024,9,640]{2,0,1:T(8,128)(2,1)} %constant_dynamic-update-slice_fusion), kind=kOutput, calls=%fused_computation.91 | convolution fusion | flops 7549747200 | bytes 27852800 | tf_op jit(solution)/shard_map/rkc,rq->ckq/dot_general | solution.py:164
  319.7 15.2 %copy.42 = f32[640,5760]{1,0:T(8,128)} copy(f32[640,5760]{0,1:T(8,128)} %bitcast.130) | data formatting | bytes 29491200 | tf_op jit(solution)/shard_map/reshape | solution.py:172
  335.1 1.4 pad_maximum_fusion.4
  336.5 3.9 fusion.15
  340.4 5.9 copy.43
  346.3 15.2 %pad_maximum_fusion = f32[640,7936]{1,0:T(8,128)} fusion(f32[640,256]{1,0:T(8,128)S(1)} %copy-done.11, f32[640,1920]{1,0:T(8,128)} %copy.43, f32[640,5760]{1,0:T(8,128)} %copy.42), kind=kLoop, calls=%fused_computation | loop fusion | flops 10158080 | bytes 40632320 | tf_op jit(solution)/shard_map/concatenate | solution.py:170
  362.4 331.0 %reduce-scatter.2.cloned.1.call-done = f32[80,7936]{1,0:T(8,128)} async-done(((f32[640,7936]{1,0:T(8,128)}), f32[80,7936]{1,0:T(8,128)}) %reduce-scatter.2.cloned.1.call-update) | async-done | bytes 2539536 | tf_op jit(solution)/shard_map/reduce_scatter | solution.py:169
  693.5 4.7 fusion.2
  698.2 0.3 pad_maximum_fusion.3
  698.5 1.7 copy-done.5
  700.2 1.8 fusion.6
  702.1 1.1 copy.44
  703.2 50.7 %all-reduce.13.cloned.1.call-done = f32[80,7936]{1,0:T(8,128)} async-done(((f32[80,7936]{1,0:T(8,128)}), f32[80,7936]{1,0:T(8,128)}) %all-reduce.13.cloned.1.call-update) | async-done | bytes 2539536 | tf_op jit(solution)/shard_map/psum | solution.py:182
  754.0 2.9 slice.165
  756.8 1.9 slice.166
  758.8 1.5 slice.167
  (70 shorter events, 2.7 us)
Async XLA Ops:
  7.2 199.8 %copy-start = (bf16[1,2,16,16,640]{4,3,2,1,0:T(8,128)(2,1)S(1)}, bf16[1,2,16,16,640]{4,3,2,1,0:T(8,128)(2,1)}, u32[]{:S(2)}) copy-start(bf16[1,2,16,16,640]{4,3,2,1,0:T(8,128)(2,1)} %param.9) | copy-start | bytes 1966084
  7.2 209.2 %all-gather.2.cloned.1.call-start = ((), (), s32[]{:S(2)}) async-start(), calls=%async_computation.1 | async-start | bytes 8294400 | tf_op jit(solution)/shard_map/all_gather | solution.py:128
  7.9 685.6 %reduce-scatter.2.cloned.1.call-start = ((), (), s32[]{:S(2)}) async-start(), calls=%async_computation.2 | async-start | bytes 22855680 | tf_op jit(solution)/shard_map/reduce_scatter | solution.py:169
  8.0 10.5 %collective-permute-start.1 = (bf16[1,80,1920]{2,1,0:T(8,128)(2,1)}, bf16[1,80,1920]{2,1,0:T(8,128)(2,1)S(1)}, u32[]{:S(2)}, u32[]{:S(2)}) collective-permute-start(bf16[1,80,1920]{2,1,0:T(8,128)(2,1)} %bitcast.163), channel_id=1, source_target_pairs={{0,4},{4,0},{8,12},{12,8},{16,20},{20,16},{24,28},{28,24},{1,5},{5... | collective-permute-start | bytes 921608 | tf_op jit(solution)/shard_map/ppermute | solution.py:27
  19.5 0.7 copy-start.6
  20.3 47.2 %copy-start.1 = (bf16[1,4,16,16,640]{4,3,2,1,0:T(8,128)(2,1)S(1)}, bf16[1,4,16,16,640]{4,3,2,1,0:T(8,128)(2,1)}, u32[]{:S(2)}) copy-start(bf16[1,4,16,16,640]{4,3,2,1,0:T(8,128)(2,1)} %param.8) | copy-start | bytes 3932164
  20.3 42.8 %collective-permute-start.2 = (bf16[2,80,1920]{2,1,0:T(8,128)(2,1)S(1)}, bf16[2,80,1920]{2,1,0:T(8,128)(2,1)}, u32[]{:S(2)}, u32[]{:S(2)}) collective-permute-start(bf16[2,80,1920]{2,1,0:T(8,128)(2,1)S(1)} %pad_maximum_fusion.6), channel_id=1, source_target_pairs={{0,8},{4,12},{8,0},{12,4},{16,24},{20,28},{24,16},{28,20},{1,9},{5... | collective-permute-start | bytes 1843208 | tf_op jit(solution)/shard_map/ppermute | solution.py:27
  64.4 5.3 copy-start.15
  65.5 132.0 %collective-permute-start.3 = (bf16[4,80,1920]{2,1,0:T(8,128)(2,1)}, bf16[4,80,1920]{2,1,0:T(8,128)(2,1)}, u32[]{:S(2)}, u32[]{:S(2)}) collective-permute-start(bf16[4,80,1920]{2,1,0:T(8,128)(2,1)} %pad_maximum_fusion.5), channel_id=1, source_target_pairs={{0,16},{4,20},{8,24},{12,28},{16,0},{20,4},{24,8},{28,12},{1,17},{... | collective-permute-start | bytes 3686408 | tf_op jit(solution)/shard_map/ppermute | solution.py:27
  210.7 4.0 collective-permute-start.4
  215.2 11.4 %copy-start.12 = (bf16[4,256,640]{2,1,0:T(8,128)(2,1)}, bf16[4,256,640]{2,1,0:T(8,128)(2,1)S(1)}, u32[]{:S(2)}) copy-start(bf16[4,256,640]{2,1,0:T(8,128)(2,1)S(1)} %get-tuple-element.38) | copy-start | bytes 3932164
  256.1 4.3 copy-start.2
  256.1 4.8 copy-start.3
  256.2 5.6 copy-start.4
  270.8 10.0 %slice-start = ((s8[7372800]{0:T(1024)(128)(4,1)}), s8[4194304]{0:T(1024)(128)(4,1)S(1)}, s32[]{:S(2)}) async-start(s8[7372800]{0:T(1024)(128)(4,1)} %bitcast.135), calls=%async_computation.4 | async-start | bytes 8388608
  271.7 4.4 copy-start.14
  276.0 4.8 slice-start.1
  280.8 24.0 %copy-start.13 = (bf16[4,256,640]{2,1,0:T(8,128)(2,1)S(1)}, bf16[4,256,640]{2,1,0:T(8,128)(2,1)}, u32[]{:S(2)}) copy-start(bf16[4,256,640]{2,1,0:T(8,128)(2,1)} %copy-done.12) | copy-start | bytes 3932164
  294.3 40.7 %collective-permute-start = (bf16[256,640]{1,0:T(8,128)(2,1)}, bf16[256,640]{1,0:T(8,128)(2,1)}, u32[]{:S(2)}, u32[]{:S(2)}) collective-permute-start(bf16[256,640]{1,0:T(8,128)(2,1)} %slice.149), channel_id=1, source_target_pairs={{0,1},{1,2},{2,3},{4,5},{5,6},{6,7},{8,9},{9,10},{10,11},{12,13},{... | collective-permute-start | bytes 983048 | tf_op jit(solution)/shard_map/ppermute | solution.py:39
  335.0 5.3 copy-start.7
  335.0 5.3 copy-start.9
  340.4 5.9 copy-start.11
  361.5 392.4 %all-reduce.13.cloned.1.call-start = ((), (), s32[]{:S(2)}) async-start(), calls=%async_computation.3 | async-start | bytes 5079040 | tf_op jit(solution)/shard_map/psum | solution.py:182
  693.5 4.7 copy-start.8
  693.5 4.7 copy-start.10
  698.2 1.9 copy-start.5
Sparse Core Ops, SparseCore 0:
  10.2 168.7 all-gather.1
  361.7 331.7 reduce-scatter.1
  696.0 57.9 all-reduce.12
